TPU v7x, 128 devices: a whole 4x4x4 slice. The times are simulated.
128 devices in a mesh: seq: 8 (over y_lo, x), dp: 16 (over y_hi, z, core).
Axes of the slice: x: 4, y: 4 (y_hi: 2, y_lo: 2; y = y_hi * 2 + y_lo), z: 4, core: 2. Of those that a mesh axis runs over, the one named last changes fastest.
Arguments:
- frames_in: bfloat16 [16, 8, 16, 320, 128], P('dp', 'seq'), may hold values from -6 to 6
- spatial_kernel: bfloat16 [9, 320, 320], P(None, 'seq'), may hold values from -0.109375 to 0.109375
- temporal_kernel: bfloat16 [3, 320, 320], P(None, 'seq'), may hold values from -0.1875 to 0.1875
- out_cotangent: bfloat16 [16, 8, 16, 320, 128], P('dp', 'seq'), may hold values from -6 to 6
Outputs:
- block_out: bfloat16 [16, 8, 16, 320, 128], P('dp', 'seq')
- input_grad: bfloat16 [16, 8, 16, 320, 128], P('dp', 'seq')
- spatial_grad: float32 [9, 320, 320], P(None, 'seq')
- temporal_grad: float32 [3, 320, 320], P(None, 'seq')
All inputs are finite; a program needn't handle non-finite values.
Results may differ from a plain program's by a relative error of at most 0.0055.
Values may be sent and summed in bfloat16 or wider, within the bound.
A program may use at most 128 MiB of HBM per device.

v0:
```python
import math

import jax
import jax.numpy as jnp
from jax import lax
from jax.sharding import PartitionSpec as P


def pad_frames(values):
    return jnp.pad(values, ((0, 0), (1, 1), (0, 0), (0, 0), (0, 0)))


def pad_pixels(values):
    return jnp.pad(values, ((0, 0), (0, 0), (1, 1), (0, 0), (1, 1)))


def spatial_forward(frames, kernel):
    row_count = frames.shape[2]
    col_count = frames.shape[4]
    padded = pad_pixels(frames)
    running = jnp.zeros(frames.shape[:3] + (kernel.shape[1], col_count), jnp.float32)
    for offset_row in range(3):
        for offset_col in range(3):
            window = padded[
                :, :, offset_row : offset_row + row_count, :, offset_col : offset_col + col_count
            ]
            running = running + jnp.einsum(
                "oc,bfhcw->bfhow",
                kernel[3 * offset_row + offset_col],
                window,
                preferred_element_type=jnp.float32,
            )
    return running


def spatial_backward(pre_grad, kernel):
    row_count = pre_grad.shape[2]
    col_count = pre_grad.shape[4]
    padded = pad_pixels(pre_grad)
    running = jnp.zeros(pre_grad.shape[:3] + (kernel.shape[2], col_count), jnp.float32)
    for offset_row in range(3):
        for offset_col in range(3):
            window = padded[
                :,
                :,
                2 - offset_row : 2 - offset_row + row_count,
                :,
                2 - offset_col : 2 - offset_col + col_count,
            ]
            running = running + jnp.einsum(
                "oc,bfhow->bfhcw",
                kernel[3 * offset_row + offset_col],
                window,
                preferred_element_type=jnp.float32,
            )
    return running


def spatial_weight_grad(frames, pre_grad):
    row_count = frames.shape[2]
    col_count = frames.shape[4]
    padded = pad_pixels(frames)
    pieces = []
    for offset_row in range(3):
        for offset_col in range(3):
            window = padded[
                :, :, offset_row : offset_row + row_count, :, offset_col : offset_col + col_count
            ]
            pieces.append(
                jnp.einsum("bfhow,bfhcw->oc", pre_grad, window, preferred_element_type=jnp.float32)
            )
    return jnp.stack(pieces)


def temporal_forward(padded_act, kernel):
    frame_count = padded_act.shape[1] - 2
    running = jnp.zeros(
        padded_act.shape[:1]
        + (frame_count,)
        + padded_act.shape[2:3]
        + (kernel.shape[1], padded_act.shape[4]),
        jnp.float32,
    )
    for offset in range(3):
        running = running + jnp.einsum(
            "oc,bfhcw->bfhow",
            kernel[offset],
            padded_act[:, offset : offset + frame_count],
            preferred_element_type=jnp.float32,
        )
    return running


def temporal_backward(padded_cot, kernel):
    frame_count = padded_cot.shape[1] - 2
    running = jnp.zeros(
        padded_cot.shape[:1]
        + (frame_count,)
        + padded_cot.shape[2:3]
        + (kernel.shape[2], padded_cot.shape[4]),
        jnp.float32,
    )
    for offset in range(3):
        running = running + jnp.einsum(
            "oc,bfhow->bfhcw",
            kernel[offset],
            padded_cot[:, 2 - offset : 2 - offset + frame_count],
            preferred_element_type=jnp.float32,
        )
    return running


def temporal_weight_grad(cotangent, padded_act):
    frame_count = cotangent.shape[1]
    pieces = []
    for offset in range(3):
        pieces.append(
            jnp.einsum(
                "bfhow,bfhcw->oc",
                cotangent,
                padded_act[:, offset : offset + frame_count],
                preferred_element_type=jnp.float32,
            )
        )
    return jnp.stack(pieces)


def local(frames_in, spatial_kernel, temporal_kernel, out_cotangent):
    spatial_full, temporal_full = (
        lax.all_gather(spatial_kernel, "seq", axis=1, tiled=True),
        lax.all_gather(temporal_kernel, "seq", axis=1, tiled=True),
    )
    pre_act = lax.optimization_barrier(
        spatial_forward(frames_in, spatial_full).astype(jnp.bfloat16)
    )
    pre_wide = pre_act.astype(jnp.float32)
    activated = jax.nn.silu(pre_wide).astype(jnp.bfloat16)
    act_rows = lax.all_to_all(activated, "seq", split_axis=2, concat_axis=1, tiled=True)
    padded_act = pad_frames(act_rows)
    temporal_rows = temporal_forward(padded_act, temporal_full).astype(jnp.bfloat16)
    temporal = lax.all_to_all(temporal_rows, "seq", split_axis=1, concat_axis=2, tiled=True)
    cot_rows = lax.all_to_all(out_cotangent, "seq", split_axis=2, concat_axis=1, tiled=True)
    grad_rows = temporal_backward(pad_frames(cot_rows), temporal_full).astype(jnp.bfloat16)
    act_grad = lax.all_to_all(grad_rows, "seq", split_axis=1, concat_axis=2, tiled=True)
    temporal_part = temporal_weight_grad(cot_rows, padded_act)
    block_out = (frames_in.astype(jnp.float32) + temporal.astype(jnp.float32)).astype(jnp.bfloat16)
    sigmoid_value = jax.nn.sigmoid(pre_wide)
    pre_grad = (
        act_grad.astype(jnp.float32) * sigmoid_value * (1.0 + pre_wide * (1.0 - sigmoid_value))
    ).astype(jnp.bfloat16)
    spatial_part = spatial_weight_grad(frames_in, pre_grad)
    input_grad = (
        out_cotangent.astype(jnp.float32) + spatial_backward(pre_grad, spatial_full)
    ).astype(jnp.bfloat16)
    clip_total = lax.axis_size("dp") * frames_in.shape[0]
    frame_total = lax.axis_size("seq") * frames_in.shape[1]
    grad_scale = 1.0 / math.sqrt(clip_total * frame_total * frames_in.shape[2] * frames_in.shape[4])
    spatial_part = spatial_part * grad_scale
    temporal_part = temporal_part * grad_scale
    replica_terms = lax.psum((spatial_part, temporal_part), "dp")
    spatial_grad, temporal_grad = (
        lax.psum_scatter(replica_terms[0], "seq", scatter_dimension=1, tiled=True),
        lax.psum_scatter(replica_terms[1], "seq", scatter_dimension=1, tiled=True),
    )
    return (block_out, input_grad, spatial_grad, temporal_grad)


def solution(mesh):
    placed = (
        P("dp", "seq", None, None, None),
        P(None, "seq", None),
        P(None, "seq", None),
        P("dp", "seq", None, None, None),
    )
    return jax.shard_map(
        local,
        mesh=mesh,
        in_specs=placed,
        out_specs=(
            P("dp", "seq", None, None, None),
            P("dp", "seq", None, None, None),
            P(None, "seq", None),
            P(None, "seq", None),
        ),
        check_vma=False,
    )
```

profile of v0, /device:TPU:1, one launch (start us, length us, event | category | flops | bytes accessed | tf_op | source)
XLA Modules:
  0.0 416.0 jit_solution(5714730043316298175)
XLA Ops:
  7.9 5.9 %all-to-all-start.2 = ((bf16[1,1,16,320,128]{4,3,1,0,2:T(8,128)(2,1)}), bf16[1,1,16,320,128]{4,3,1,0,2:T(8,128)(2,1)S(1)}, u32[]{:S(2)}, u32[]{:S(2)}) async-start(bf16[1,1,16,320,128]{4,3,1,0,2:T(8,128)(2,1)} %bitcast.350), calls=%async_computation.2 | async-start | bytes 2621440 | tf_op jit(solution)/shard_map/all_to_all | solution.py:142
  13.8 46.7 %all_gather.7 = bf16[3,320,320]{2,1,0:T(8,128)(2,1)S(1)} all-gather(bf16[3,40,320]{2,1,0:T(8,128)(2,1)S(1)} %copy-done.6), channel_id=1, replica_groups=mesh['seq'=8,'dp'=16] {'seq'}, dimensions={1}, use_global_device_ids=true | all-gather | bytes 691200 | tf_op jit(solution)/shard_map/all_gather | solution.py:131
  62.2 2.0 fusion.10
  64.2 3.9 all-to-all-start.3
  68.2 1.9 fusion.148
  71.0 0.9 fusion.154
  72.8 0.9 fusion.157
  76.6 2.7 fusion.11
  79.2 4.8 %all-to-all-done.3 = bf16[1,8,2,320,128]{4,3,2,0,1:T(8,128)(2,1)S(1)} async-done(((bf16[1,8,2,320,128]{4,3,2,0,1:T(8,128)(2,1)}), bf16[1,8,2,320,128]{4,3,2,0,1:T(8,128)(2,1)S(1)}, u32[]{:S(2)}, u32[]{:S(2)}) %all-to-all-start.3) | async-done | bytes 1310752 | tf_op jit(solution)/shard_map/all_to_all | solution.py:144
  84.0 1.1 copy-done.5
  85.1 4.1 fusion.6
  89.2 4.3 %all-to-all-start = ((bf16[1,1,16,320,128]{4,3,1,0,2:T(8,128)(2,1)}), bf16[1,1,16,320,128]{4,3,1,0,2:T(8,128)(2,1)}, u32[]{:S(2)}, u32[]{:S(2)}) async-start(bf16[1,1,16,320,128]{4,3,1,0,2:T(8,128)(2,1)} %get-tuple-element.15), calls=%async_computation | async-start | bytes 2621440 | tf_op jit(solution)/shard_map/all_to_all | solution.py:138
  93.7 1.8 fusion.80
  95.5 1.7 fusion.86
  97.1 1.7 fusion.92
  98.8 1.7 fusion.98
  100.6 1.6 fusion.106
  102.2 1.7 fusion.114
  103.9 8.1 %all-to-all-done = bf16[1,1,16,320,128]{4,3,1,0,2:T(8,128)(2,1)} async-done(((bf16[1,1,16,320,128]{4,3,1,0,2:T(8,128)(2,1)}), bf16[1,1,16,320,128]{4,3,1,0,2:T(8,128)(2,1)}, u32[]{:S(2)}, u32[]{:S(2)}) %all-to-all-start) | async-done | bytes 1310752 | tf_op jit(solution)/shard_map/all_to_all | solution.py:138
  112.1 2.6 convolution_bitcast_fusion.1
  114.7 2.1 convolution_bitcast_fusion
  116.8 2.2 fusion.135
  119.0 1.3 maximum_multiply_fusion
  120.3 3.7 copy.37
  124.3 1.7 fusion.120
  126.0 1.7 fusion.126
  127.7 1.8 fusion.132
  129.4 4.8 %broadcast_multiply_fusion = f32[9,320,320]{2,1,0:T(8,128)} fusion(f32[9,320,320]{2,1,0:T(8,128)} %fusion.132), kind=kLoop, calls=%fused_computation.34 | loop fusion | flops 921600 | bytes 7372800 | tf_op jit(solution)/shard_map/mul | solution.py:158
  136.1 3.5 fusion.32
  139.7 2.5 fusion.35
  142.2 2.5 fusion.38
  144.7 2.5 fusion.41
  147.2 2.6 fusion.44
  149.8 2.4 fusion.47
  152.2 2.5 fusion.29
  154.7 2.4 fusion.72
  157.1 2.1 fusion.143
  159.1 2.1 fusion.169
  161.3 3.2 fusion.9
  164.5 4.3 %all-to-all-start.1 = ((bf16[1,8,2,320,128]{4,3,2,0,1:T(8,128)(2,1)}), bf16[1,8,2,320,128]{4,3,2,0,1:T(8,128)(2,1)}, u32[]{:S(2)}, u32[]{:S(2)}) async-start(bf16[1,8,2,320,128]{4,3,2,0,1:T(8,128)(2,1)} %fusion.9), calls=%async_computation.1 | async-start | bytes 2621440 | tf_op jit(solution)/shard_map/all_to_all | solution.py:141
  169.1 41.4 %all-reduce.9.cloned.1.call-done = f32[3,320,320]{2,0,1:T(4,128)} async-done(((f32[3,320,320]{2,0,1:T(4,128)}), f32[3,320,320]{2,0,1:T(4,128)}) %all-reduce.9.cloned.1.call-update) | async-done | bytes 1228816
  210.5 1.7 constant_dynamic-slice_fusion
  212.2 55.2 %reduce-scatter.2.cloned.1.call-done = f32[9,40,320]{2,1,0:T(8,128)} async-done(((f32[9,320,320]{2,1,0:T(8,128)}), f32[9,40,320]{2,1,0:T(8,128)}) %reduce-scatter.2.cloned.1.call-update) | async-done | bytes 460816 | tf_op jit(solution)/shard_map/reduce_scatter | solution.py:162
  267.3 10.5 %fusion.7 = bf16[1,1,16,320,128]{4,3,2,1,0:T(8,128)(2,1)} fusion(f32[16,128,320]{1,2,0:T(8,128)} %fusion.47, f32[16,128,320]{1,2,0:T(8,128)} %fusion.44, f32[16,128,320]{1,2,0:T(8,128)} %fusion.41, f32[16,128,320]{1,2,0:T(8,128)} %fusion.72, f32[16,128,320]{1,2,0:T(8,128)} %fusion.38, f32[16,128,320]{1,2,0:T(8,128)} %fusion.35, ...), kind=kOutput, calls=%fused_computation.27 | convolution fusion | flops 426639360 | bytes 25149440 | tf_op jit(solution)/shard_map/oc,bfhow->bfhcw/dot_general | solution.py:50
  277.8 2.7 fusion.8
  280.5 125.4 %all-reduce.11.cloned.1.call-done = (f32[9,40,320]{2,1,0:T(8,128)}, f32[3,40,320]{2,0,1:T(4,128)}) async-done(((f32[9,40,320]{2,1,0:T(8,128)}, f32[3,40,320]{2,0,1:T(4,128)}), (f32[9,40,320]{2,1,0:T(8,128)}, f32[3,40,320]{2,0,1:T(4,128)})) %all-reduce.11.cloned.1.call-update) | async-done | bytes 614416 | tf_op jit(solution)/shard_map/psum | solution.py:160
  406.0 1.6 copy.38
  407.6 1.9 copy.79
  (34 shorter events, 9.2 us)
Async XLA Ops:
  7.2 6.6 %copy-start.6 = (bf16[3,40,320]{2,1,0:T(8,128)(2,1)S(1)}, bf16[3,40,320]{2,1,0:T(8,128)(2,1)}, u32[]{:S(2)}) copy-start(bf16[3,40,320]{2,1,0:T(8,128)(2,1)} %param.6) | copy-start | bytes 230404
  7.2 61.0 %all-gather.2.cloned.1.call-start = ((), (), s32[]{:S(2)}) async-start(), calls=%async_computation.5 | async-start | bytes 2488320 | tf_op jit(solution)/shard_map/all_gather | solution.py:130
  7.9 52.5 %all-to-all-start.2 = ((bf16[1,1,16,320,128]{4,3,1,0,2:T(8,128)(2,1)}), bf16[1,1,16,320,128]{4,3,1,0,2:T(8,128)(2,1)S(1)}, u32[]{:S(2)}, u32[]{:S(2)}) async-start(bf16[1,1,16,320,128]{4,3,1,0,2:T(8,128)(2,1)} %bitcast.350), calls=%async_computation.2 | async-start | bytes 2621440 | tf_op jit(solution)/shard_map/all_to_all | solution.py:142
  60.5 1.8 copy-start.1
  64.2 3.9 copy-start
  64.2 19.8 %all-to-all-start.3 = ((bf16[1,8,2,320,128]{4,3,2,0,1:T(8,128)(2,1)}), bf16[1,8,2,320,128]{4,3,2,0,1:T(8,128)(2,1)S(1)}, u32[]{:S(2)}, u32[]{:S(2)}) async-start(bf16[1,8,2,320,128]{4,3,2,0,1:T(8,128)(2,1)} %fusion.10), calls=%async_computation.3 | async-start | bytes 2621440 | tf_op jit(solution)/shard_map/all_to_all | solution.py:144
  68.2 1.9 copy-start.3
  84.0 1.1 copy-start.5
  89.2 22.9 %all-to-all-start = ((bf16[1,1,16,320,128]{4,3,1,0,2:T(8,128)(2,1)}), bf16[1,1,16,320,128]{4,3,1,0,2:T(8,128)(2,1)}, u32[]{:S(2)}, u32[]{:S(2)}) async-start(bf16[1,1,16,320,128]{4,3,1,0,2:T(8,128)(2,1)} %get-tuple-element.15), calls=%async_computation | async-start | bytes 2621440 | tf_op jit(solution)/shard_map/all_to_all | solution.py:138
  93.4 117.0 %all-reduce.9.cloned.1.call-start = ((), (), s32[]{:S(2)}) async-start(), calls=%async_computation.7 | async-start | bytes 3932160
  112.1 2.6 copy-start.2
  124.0 143.3 %reduce-scatter.2.cloned.1.call-start = ((), (), s32[]{:S(2)}) async-start(), calls=%async_computation.6 | async-start | bytes 4976640 | tf_op jit(solution)/shard_map/reduce_scatter | solution.py:162
  134.2 0.7 copy-start.7
  136.1 3.5 copy-start.4
  164.5 113.3 %all-to-all-start.1 = ((bf16[1,8,2,320,128]{4,3,2,0,1:T(8,128)(2,1)}), bf16[1,8,2,320,128]{4,3,2,0,1:T(8,128)(2,1)}, u32[]{:S(2)}, u32[]{:S(2)}) async-start(bf16[1,8,2,320,128]{4,3,2,0,1:T(8,128)(2,1)} %fusion.9), calls=%async_computation.1 | async-start | bytes 2621440 | tf_op jit(solution)/shard_map/all_to_all | solution.py:141
  168.7 237.2 %all-reduce.11.cloned.1.call-start = ((), (), s32[]{:S(2)}) async-start(), calls=%async_computation.8 | async-start | bytes 1597440 | tf_op jit(solution)/shard_map/psum | solution.py:160
Sparse Core Ops, SparseCore 0:
  9.7 50.1 all-gather.1
  124.1 86.3 all-reduce.8
  213.0 54.2 reduce-scatter.1
  270.5 135.4 all-reduce.10
where the time goes:
time: 417 us; the launch traced here: 416 us
  waiting for transfers between devices  236 us (57%)
  matrix products  75.9 us (18%)
  blocking collectives  46.7 us (11%)
  starting transfers between devices  19.2 us (5%)
  between operations  14.6 us (4%)
  other arithmetic  12.9 us (3%)
  local copies, waits for them, and re-layouts  11.1 us (3%)
    psum x1, waiting for transfers between devices, local(): replica_terms = lax.psum((spatial_part, temporal_part), 'dp')  125 us
    reduce_scatter x1, waiting for transfers between devices, local(): lax.psum_scatter(replica_terms[0], 'seq', scatter_dimension=1, tiled=True)  55.2 us
    all_gather x1, blocking collectives, local(): lax.all_gather(temporal_kernel, 'seq', axis=1, tiled=True)  46.7 us
    unnamed x5, waiting for transfers between devices  42.1 us
    dot_general x9, matrix products, spatial_backward(): jnp.einsum('oc,bfhow->bfhcw', kernel[3 * offset_row + offset_col], window...  31.4 us
    dot_general x9, matrix products, spatial_weight_grad(): jnp.einsum('bfhow,bfhcw->oc', pre_grad, window, preferred_element_type=jn...  15.4 us
    dot_general x9, matrix products, spatial_forward(): jnp.einsum('oc,bfhcw->bfhow', kernel[3 * offset_row + offset_col], window...  11 us
  transfers between devices with their start and end apart: 8, of which 5 were waited for; matrix products, arithmetic and copies ran while one was open for 19% of the time, Pallas kernels for 0%

commit v1 on v0

v1 whole, which is shorter than its diff:
```python
import math

import jax
import jax.numpy as jnp
from jax import lax
from jax.experimental import pallas as pl
from jax.experimental.pallas import tpu as pltpu
from jax.sharding import PartitionSpec as P

MESH = pl.DeviceIdType.MESH
ROWS, CH, COLS = 16, 320, 128
PAIRS = ROWS // 2
SHARD = CH // 8
SLAB = 3 * CH
WIDE = 1024
BF16, F32 = jnp.bfloat16, jnp.float32


def remote(src, dst, send_sem, recv_sem, device):
    return pltpu.make_async_remote_copy(
        src_ref=src,
        dst_ref=dst,
        send_sem=send_sem,
        recv_sem=recv_sem,
        device_id=device,
        device_id_type=MESH,
    )


def dot(lhs, rhs):
    return jnp.dot(lhs, rhs, preferred_element_type=F32)


def dot_pixels(lhs, rhs):
    return lax.dot_general(lhs, rhs, (((1,), (1,)), ((), ())), preferred_element_type=F32)


def shifted(value, offset):
    column = lax.broadcasted_iota(jnp.int32, value.shape, 1)
    rolled = pltpu.roll(value, (-offset) % COLS, 1)
    edge = 0 if offset < 0 else COLS - 1
    return jnp.where(column == edge, 0.0, rolled)


def body(
    frames_hbm, spatial_ref, temporal_ref, cot_hbm,
    block_hbm, input_hbm, sgrad_ref, tgrad_ref,
    frames, cot3, act3, pre, xs, pgs, wsrc, wall, wl, wt,
    part, cs, cr, ys, yr, zs, zr, hold, hx, xr, hs, hr, final,
    out_block, out_input,
    load_sem, store_sem,
    cot_send, cot_recv, act_send, act_recv,
    wx_send, wx_recv, wz_send, wz_recv, wy_send, wy_recv, wc_send, wc_recv,
    gc_send, gc_recv, gy_send, gy_recv, gz_send, gz_recv, gx_send, gx_recv,
    gh_send, gh_recv, fz_send, fz_recv, fc_send, fc_recv,
):
    s = lax.axis_index("seq")
    d = lax.axis_index("dp")
    x, ylo = s % 4, s // 4
    core, z, yhi = d % 2, (d // 2) % 4, d // 8
    y = 2 * yhi + ylo

    def device(x_, y_, z_, core_):
        return {"seq": (y_ % 2) * 4 + x_, "dp": (y_ // 2) * 8 + z_ * 2 + core_}

    def along_x(offset):
        return device((x + offset) % 4, y, z, core)

    def along_y(offset):
        return device(x, (y + offset) % 4, z, core)

    def along_z(offset):
        return device(x, y, (z + offset) % 4, core)

    partner = device(x, y, z, 1 - core)
    right = {"seq": jnp.minimum(s + 1, 7), "dp": d}
    left = {"seq": jnp.maximum(s - 1, 0), "dp": d}
    has_right, has_left = s < 7, s > 0
    mine = x // 2 == core

    load_frames = pltpu.make_async_copy(frames_hbm, frames, load_sem.at[0])
    load_cot = pltpu.make_async_copy(cot_hbm, cot3.at[1], load_sem.at[1])
    load_frames.start()
    load_cot.start()

    barrier = pltpu.get_barrier_semaphore()
    for offset in (1, 2, 3):
        for peer in (along_x(offset), along_y(offset), along_z(offset)):
            pl.semaphore_signal(barrier, inc=1, device_id=peer, device_id_type=MESH)
    pl.semaphore_signal(barrier, inc=1, device_id=partner, device_id_type=MESH)

    @pl.when(s == 3)
    def _():
        pl.semaphore_signal(barrier, inc=1, device_id=right, device_id_type=MESH)

    @pl.when(s == 4)
    def _():
        pl.semaphore_signal(barrier, inc=1, device_id=left, device_id_type=MESH)

    for q in range(3):
        wsrc[q] = jnp.concatenate(
            [spatial_ref[3 * a + q].astype(F32) for a in range(3)], axis=1
        ).astype(BF16)
    wsrc[3] = jnp.concatenate(
        [temporal_ref[k].astype(F32) for k in range(3)], axis=1
    ).astype(BF16)

    pl.semaphore_wait(barrier, jnp.where(jnp.logical_or(s == 3, s == 4), 11, 10))

    def weight_x(offset):
        return remote(
            wsrc.at[z], wall.at[z, ylo, x], wx_send.at[offset], wx_recv.at[offset], along_x(offset)
        )

    @pl.when(mine)
    def _():
        wall[z, ylo, x] = wsrc[z]
        for offset in (1, 3, 2):
            weight_x(offset).start()

    def halo(source, slots, pair, to_right, send, recv):
        rows = pl.ds(2 * pair, 2)
        slot, side, target = (0, 0, right) if to_right else (2, 1, left)
        return remote(
            source.at[rows],
            slots.at[slot, rows],
            send.at[side, pair],
            recv.at[side, pair],
            target,
        )

    load_cot.wait()

    def send_cot(pair, carry):
        @pl.when(has_right)
        def _():
            halo(cot3.at[1], cot3, pair, True, cot_send, cot_recv).start()

        @pl.when(has_left)
        def _():
            halo(cot3.at[1], cot3, pair, False, cot_send, cot_recv).start()

        return carry

    lax.fori_loop(0, PAIRS, send_cot, 0)

    load_frames.wait()
    for b in range(3):
        xs[b, pl.ds(0, CH), :] = jnp.zeros((CH, COLS), BF16)
        xs[b, pl.ds(17 * CH, 2 * CH), :] = jnp.zeros((2 * CH, COLS), BF16)
        pgs[b, pl.ds(0, CH), :] = jnp.zeros((CH, COLS), BF16)
        pgs[b, pl.ds(17 * CH, CH), :] = jnp.zeros((CH, COLS), BF16)

    def shift_frames(row, carry):
        value = frames[row]
        wide = value.astype(F32)
        place = pl.ds(pl.multiple_of((row + 1) * CH, 64), CH)
        xs[0, place, :] = shifted(wide, -1).astype(BF16)
        xs[1, place, :] = value
        xs[2, place, :] = shifted(wide, 1).astype(BF16)
        return carry

    lax.fori_loop(0, ROWS, shift_frames, 0)

    @pl.when(s == 0)
    def _():
        cot3[0] = jnp.zeros((ROWS, CH, COLS), BF16)
        act3[0] = jnp.zeros((ROWS, CH, COLS), BF16)

    @pl.when(s == 7)
    def _():
        cot3[2] = jnp.zeros((ROWS, CH, COLS), BF16)
        act3[2] = jnp.zeros((ROWS, CH, COLS), BF16)

    both = pl.ds(2 * core, 2)
    for offset in (1, 3, 2):
        @pl.when((x + 4 - offset) % 4 // 2 == core)
        def _():
            weight_x(offset).wait_recv()

    def weight_z(offset):
        chunk = wall.at[z, ylo, both]
        return remote(chunk, chunk, wz_send.at[offset], wz_recv.at[offset], along_z(offset))

    def weight_y(q, index):
        chunk = wall.at[q, ylo, both]
        target = along_y(jnp.where(q < 2, 1, 3))
        return remote(chunk, chunk, wy_send.at[index], wy_recv.at[index], target)

    def weight_core(q, index):
        chunk = wall.at[q, :, both]
        return remote(chunk, chunk, wc_send.at[index], wc_recv.at[index], partner)

    for offset in (1, 3, 2):
        weight_z(offset).start()
    order = (0, 1, 3, 2)
    for index in order:
        q = (z + 4 - index) % 4
        if index:
            weight_z(index).wait_recv()
        weight_y(q, index).start()
    for index in order:
        weight_y((z + 4 - index) % 4, index).wait_recv()
        weight_core((z + 4 - index) % 4, index).start()
    for index in order:
        weight_core((z + 4 - index) % 4, index).wait_recv()

    def place_weights(q, carry):
        full = jnp.concatenate(
            [wall[q, owner // 4, owner % 4].astype(F32) for owner in range(8)], axis=0
        )
        wl[q] = full.astype(BF16)
        turned = full.T
        wt[q] = jnp.concatenate(
            [turned[CH * a : CH * a + CH] for a in (2, 1, 0)], axis=1
        ).astype(BF16)
        return carry

    lax.fori_loop(0, 4, place_weights, 0)

    def slab_pair(ref, pair):
        first = pl.multiple_of(2 * pair * CH, 128)
        return jnp.concatenate(
            [ref[pl.ds(first, SLAB), :], ref[pl.ds(pl.multiple_of(first + CH, 64), SLAB), :]], axis=1
        )

    def frame_pair(ref, pair):
        return jnp.concatenate(
            [
                jnp.concatenate([ref[k, 2 * pair + i] for k in range(3)], axis=0)
                for i in range(2)
            ],
            axis=1,
        )

    def forward(pair, carry):
        total = dot(wl[0], slab_pair(xs.at[0], pair))
        total += dot(wl[1], slab_pair(xs.at[1], pair))
        total += dot(wl[2], slab_pair(xs.at[2], pair))
        rounded = total.astype(BF16)
        wide = rounded.astype(F32)
        activated = (wide / (1.0 + jnp.exp(-wide))).astype(BF16)
        for i in range(2):
            pre[2 * pair + i] = rounded[:, COLS * i : COLS * i + COLS]
            act3[1, 2 * pair + i] = activated[:, COLS * i : COLS * i + COLS]

        @pl.when(has_right)
        def _():
            halo(act3.at[1], act3, pair, True, act_send, act_recv).start()

        @pl.when(has_left)
        def _():
            halo(act3.at[1], act3, pair, False, act_send, act_recv).start()

        return carry

    lax.fori_loop(0, PAIRS, forward, 0)

    def wait_halo(slots, pair, send, recv):
        @pl.when(has_left)
        def _():
            halo(slots.at[1], slots, pair, True, send, recv).wait_recv()

        @pl.when(has_right)
        def _():
            halo(slots.at[1], slots, pair, False, send, recv).wait_recv()

    def backward(pair, carry):
        wait_halo(cot3, pair, cot_send, cot_recv)
        grad = dot(wt[3], frame_pair(cot3, pair)).astype(BF16)
        for i in range(2):
            row = 2 * pair + i
            act_grad = grad[:, COLS * i : COLS * i + COLS].astype(F32)
            wide = pre[row].astype(F32)
            sig = 1.0 / (1.0 + jnp.exp(-wide))
            value = (act_grad * sig * (1.0 + wide * (1.0 - sig))).astype(BF16)
            wide_value = value.astype(F32)
            place = pl.ds(pl.multiple_of((row + 1) * CH, 64), CH)
            pgs[0, place, :] = shifted(wide_value, 1).astype(BF16)
            pgs[1, place, :] = value
            pgs[2, place, :] = shifted(wide_value, -1).astype(BF16)
        return carry

    lax.fori_loop(0, PAIRS, backward, 0)

    def put(q, start, value, lanes):
        part[q, :, :, pl.ds(start, lanes)] = value.reshape(8, SHARD, lanes)

    def columns(ref, k):
        return [
            jnp.concatenate([ref[k, 2 * j], ref[k, 2 * j + 1]], axis=1) for j in range(PAIRS)
        ]

    def temporal_part(k, carry):
        low = jnp.zeros((CH, 256), F32)
        high = jnp.zeros((CH, 128), F32)
        for j in range(PAIRS):
            lhs = jnp.concatenate([cot3[k, 2 * j], cot3[k, 2 * j + 1]], axis=1)
            rhs = jnp.concatenate([act3[1, 2 * j], act3[1, 2 * j + 1]], axis=1)
            low += dot_pixels(lhs, rhs[:256])
            high += dot_pixels(lhs, rhs[192:])
        part[3, :, :, pl.ds(pl.multiple_of(256 * k, 128), 256)] = low.reshape(8, SHARD, 256)
        hold[k] = high
        return carry

    lax.fori_loop(0, 3, temporal_part, 0)
    lane = lax.broadcasted_iota(jnp.int32, (CH, 128), 1)
    put(3, 768, jnp.where(lane < 64, pltpu.roll(hold[0], 64, 1), hold[1]), 128)
    put(3, 896, pltpu.roll(hold[2], 64, 1), 128)

    def spatial_part(b):
        def block(n, carry):
            total = jnp.zeros((CH, 256), F32)
            for j in range(PAIRS):
                lhs = jnp.concatenate(
                    [
                        pgs[b, pl.ds((2 * j + 1) * CH, CH), :],
                        pgs[b, pl.ds((2 * j + 2) * CH, CH), :],
                    ],
                    axis=1,
                )
                base = pl.multiple_of(n * 256, 256)
                rhs = jnp.concatenate(
                    [
                        xs[1, pl.ds(base + 2 * j * CH, 256), :],
                        xs[1, pl.ds(base + (2 * j + 1) * CH, 256), :],
                    ],
                    axis=1,
                )
                total += dot_pixels(lhs, rhs)
            part[b, :, :, pl.ds(pl.multiple_of(n * 256, 256), 256)] = total.reshape(8, SHARD, 256)
            return carry

        lax.fori_loop(0, 4, block, 0)

    def owned(q, half, pair_core):
        return part[q, pl.ds(4 * half + 2 * pair_core, 2)]

    def grad_core(q):
        return remote(cs.at[q], cr.at[q], gc_send.at[q], gc_recv.at[q], partner)

    def grad_y(q):
        return remote(ys.at[q], yr.at[q], gy_send.at[q], gy_recv.at[q], along_y(1 if q < 2 else 3))

    def grad_z(q):
        offset = (q + 4 - z) % 4
        return remote(
            zs.at[q], zr.at[offset], gz_send.at[offset], gz_recv.at[offset],
            device(x, y, q, core),
        )

    def start_core(q):
        for half in range(2):
            cs[q, half] = owned(q, half, 1 - core).astype(BF16)
        grad_core(q).start()

    def core_to_y(q):
        grad_core(q).wait_recv()
        for half in range(2):
            place = pl.ds(4 * half + 2 * core, 2)
            part[q, place] = part[q, place] + cr[q, half].astype(F32)
        ys[q] = owned(q, 1 - ylo, core).astype(BF16)
        grad_y(q).start()

    def y_to_z(q):
        grad_y(q).wait_recv()
        place = pl.ds(4 * ylo + 2 * core, 2)
        part[q, place] = part[q, place] + yr[q].astype(F32)

        @pl.when(z != q)
        def _():
            zs[q] = part[q, place].astype(BF16)
            grad_z(q).start()

    def wait_z(offset):
        remote(
            zs.at[0], zr.at[offset], gz_send.at[offset], gz_recv.at[offset], along_z(offset)
        ).wait_recv()

    def grad_x(i):
        owner = 2 * core + i
        offset = (owner + 4 - x) % 4
        return remote(
            hx.at[i], xr.at[offset], gx_send.at[offset], gx_recv.at[offset],
            device(owner, y, z, core),
        )

    def z_to_x():
        total = part[z, pl.ds(4 * ylo + 2 * core, 2)]
        for offset in (1, 2, 3):
            wait_z(offset)
            total = total + zr[offset].astype(F32)
        part[z, pl.ds(4 * ylo + 2 * core, 2)] = total
        hx[...] = total.astype(BF16)
        for i in range(2):
            @pl.when(2 * core + i != x)
            def _():
                grad_x(i).start()

    grad_h = remote(hs, hr, gh_send.at[0], gh_recv.at[0], along_y(2))

    def x_to_h():
        @pl.when(mine)
        def _():
            total = part[z, s]
            for offset in (1, 2, 3):
                remote(
                    hx.at[0], xr.at[offset], gx_send.at[offset], gx_recv.at[offset],
                    along_x(offset),
                ).wait_recv()
                total = total + xr[offset].astype(F32)
            hs[...] = total.astype(BF16)
            grad_h.start()

    def final_z(offset):
        return remote(
            final.at[z], final.at[z], fz_send.at[offset], fz_recv.at[offset], along_z(offset)
        )

    def h_to_final():
        @pl.when(mine)
        def _():
            grad_h.wait_recv()
            final[z] = hs[...].astype(F32) + hr[...].astype(F32)
            for offset in (1, 3, 2):
                final_z(offset).start()

    final_core = remote(final, final, fc_send.at[0], fc_recv.at[0], partner)

    def final_to_core():
        @pl.when(mine)
        def _():
            for offset in (1, 3, 2):
                final_z(offset).wait_recv()
            final_core.start()

    start_core(3)
    spatial_part(0)
    start_core(0)
    core_to_y(3)
    spatial_part(1)
    start_core(1)
    core_to_y(0)
    y_to_z(3)
    spatial_part(2)
    start_core(2)
    core_to_y(1)
    y_to_z(0)

    def store_rows(source, target, pair, which):
        rows = pl.ds(2 * pair, 2)
        return pltpu.make_async_copy(source.at[rows], target.at[rows], store_sem.at[which, pair])

    def input_grad(pair, carry):
        total = dot(wt[0], slab_pair(pgs.at[0], pair))
        total += dot(wt[1], slab_pair(pgs.at[1], pair))
        total += dot(wt[2], slab_pair(pgs.at[2], pair))
        for i in range(2):
            row = 2 * pair + i
            value = cot3[1, row].astype(F32) + total[:, COLS * i : COLS * i + COLS]
            out_input[row] = value.astype(BF16)
        store_rows(out_input, input_hbm, pair, 0).start()

        @pl.when(pair == 1)
        def _():
            core_to_y(2)
            y_to_z(1)

        @pl.when(pair == 5)
        def _():
            y_to_z(2)

        return carry

    lax.fori_loop(0, PAIRS, input_grad, 0)

    z_to_x()

    def temporal(pair, carry):
        wait_halo(act3, pair, act_send, act_recv)
        value = dot(wl[3], frame_pair(act3, pair)).astype(BF16).astype(F32)
        for i in range(2):
            row = 2 * pair + i
            total = frames[row].astype(F32) + value[:, COLS * i : COLS * i + COLS]
            out_block[row] = total.astype(BF16)
        store_rows(out_block, block_hbm, pair, 1).start()

        @pl.when(pair == 2)
        def _():
            x_to_h()

        @pl.when(pair == 4)
        def _():
            h_to_final()

        @pl.when(pair == 6)
        def _():
            final_to_core()

        return carry

    lax.fori_loop(0, PAIRS, temporal, 0)

    @pl.when(jnp.logical_not(mine))
    def _():
        final_core.wait_recv()

    scale = 1.0 / math.sqrt(16 * 8 * ROWS * COLS)
    for b in range(3):
        value = final[b] * scale
        for a in range(3):
            sgrad_ref[3 * a + b] = value[:, CH * a : CH * a + CH]
    value = final[3] * scale
    for slot in range(3):
        tgrad_ref[2 - slot] = jnp.concatenate(
            [
                value[:, 256 * slot : 256 * slot + 256],
                value[:, 768 + 64 * slot : 768 + 64 * slot + 64],
            ],
            axis=1,
        )

    def drain(pair, carry):
        @pl.when(has_right)
        def _():
            halo(cot3.at[1], cot3, pair, True, cot_send, cot_recv).wait_send()
            halo(act3.at[1], act3, pair, True, act_send, act_recv).wait_send()

        @pl.when(has_left)
        def _():
            halo(cot3.at[1], cot3, pair, False, cot_send, cot_recv).wait_send()
            halo(act3.at[1], act3, pair, False, act_send, act_recv).wait_send()

        store_rows(out_input, input_hbm, pair, 0).wait()
        store_rows(out_block, block_hbm, pair, 1).wait()
        return carry

    lax.fori_loop(0, PAIRS, drain, 0)

    @pl.when(mine)
    def _():
        for offset in (1, 2, 3):
            weight_x(offset).wait_send()
            final_z(offset).wait_send()
        grad_h.wait_send()
        final_core.wait_send()

    for offset in (1, 2, 3):
        weight_z(offset).wait_send()
    for index in range(4):
        q = (z + 4 - index) % 4
        weight_y(q, index).wait_send()
        weight_core(q, index).wait_send()
        grad_core(index).wait_send()
        grad_y(index).wait_send()

        @pl.when(z != index)
        def _():
            grad_z(index).wait_send()

    for i in range(2):
        @pl.when(2 * core + i != x)
        def _():
            grad_x(i).wait_send()


def local(frames_in, spatial_kernel, temporal_kernel, out_cotangent):
    image = (ROWS, CH, COLS)
    dma = pltpu.SemaphoreType.DMA
    anywhere = pl.BlockSpec(memory_space=pl.ANY)
    vmem = pl.BlockSpec(memory_space=pltpu.VMEM)
    chunk = (SHARD, WIDE)
    block_out, input_grad, spatial_grad, temporal_grad = pl.pallas_call(
        body,
        out_shape=(
            jax.ShapeDtypeStruct(image, BF16),
            jax.ShapeDtypeStruct(image, BF16),
            jax.ShapeDtypeStruct((9, SHARD, CH), F32),
            jax.ShapeDtypeStruct((3, SHARD, CH), F32),
        ),
        in_specs=[anywhere, vmem, vmem, anywhere],
        out_specs=[anywhere, anywhere, vmem, vmem],
        scratch_shapes=[
            pltpu.VMEM(image, BF16),
            pltpu.VMEM((3,) + image, BF16),
            pltpu.VMEM((3,) + image, BF16),
            pltpu.VMEM(image, BF16),
            pltpu.VMEM((3, 19 * CH, COLS), BF16),
            pltpu.VMEM((3, 18 * CH, COLS), BF16),
            pltpu.VMEM((4, SHARD, SLAB), BF16),
            pltpu.VMEM((4, 2, 4, SHARD, SLAB), BF16),
            pltpu.VMEM((4, CH, SLAB), BF16),
            pltpu.VMEM((4, CH, SLAB), BF16),
            pltpu.VMEM((4, 8) + chunk, F32),
            pltpu.VMEM((4, 2, 2) + chunk, BF16),
            pltpu.VMEM((4, 2, 2) + chunk, BF16),
            pltpu.VMEM((4, 2) + chunk, BF16),
            pltpu.VMEM((4, 2) + chunk, BF16),
            pltpu.VMEM((4, 2) + chunk, BF16),
            pltpu.VMEM((4, 2) + chunk, BF16),
            pltpu.VMEM((3, CH, 128), F32),
            pltpu.VMEM((2,) + chunk, BF16),
            pltpu.VMEM((4,) + chunk, BF16),
            pltpu.VMEM(chunk, BF16),
            pltpu.VMEM(chunk, BF16),
            pltpu.VMEM((4,) + chunk, F32),
            pltpu.VMEM(image, BF16),
            pltpu.VMEM(image, BF16),
            dma((2,)),
            dma((2, PAIRS)),
            dma((2, PAIRS)), dma((2, PAIRS)), dma((2, PAIRS)), dma((2, PAIRS)),
            dma((4,)), dma((4,)), dma((4,)), dma((4,)),
            dma((4,)), dma((4,)), dma((4,)), dma((4,)),
            dma((4,)), dma((4,)), dma((4,)), dma((4,)),
            dma((4,)), dma((4,)), dma((4,)), dma((4,)),
            dma((1,)), dma((1,)), dma((4,)), dma((4,)), dma((1,)), dma((1,)),
        ],
        compiler_params=pltpu.CompilerParams(
            collective_id=0, has_side_effects=True, vmem_limit_bytes=67043328
        ),
        name="block",
    )(frames_in[0, 0], spatial_kernel, temporal_kernel, out_cotangent[0, 0])
    return block_out[None, None], input_grad[None, None], spatial_grad, temporal_grad


def solution(mesh):
    placed = (
        P("dp", "seq", None, None, None),
        P(None, "seq", None),
        P(None, "seq", None),
        P("dp", "seq", None, None, None),
    )
    return jax.shard_map(
        local,
        mesh=mesh,
        in_specs=placed,
        out_specs=(
            P("dp", "seq", None, None, None),
            P("dp", "seq", None, None, None),
            P(None, "seq", None),
            P(None, "seq", None),
        ),
        check_vma=False,
    )
```

time: 417 us -> 125 us (0.30)
  waiting for transfers between devices: 236 us -> 0 us
  Pallas kernels: 0 us -> 119 us
  matrix products: 75.9 us -> 0 us
  blocking collectives: 46.7 us -> 0 us
  starting transfers between devices: 19.2 us -> 0 us
  between operations: 14.6 us -> 0.65 us
  other arithmetic: 12.9 us -> 0 us
  local copies, waits for them, and re-layouts: 11.1 us -> 5.46 us
    psum x1 -> x0, waiting for transfers between devices: 125 us -> none  [local(): replica_terms = lax.psum((spatial_part, temporal_part), 'dp')]
    pallas_call x0 -> x1, Pallas kernels: none -> 119 us  [local(): pl.pallas_call(body, out_shape=(jax.ShapeDtypeStruct(image, BF16), jax.Sh...]
    dot_general x36 -> x0, matrix products: 75.9 us -> none  [the longest x9 31.4 us: spatial_backward(): jnp.einsum('oc,bfhow->bfhcw', kernel[3 * offset_row + offset_col], window...]
    reduce_scatter x1 -> x0, waiting for transfers between devices: 55.2 us -> none  [local(): lax.psum_scatter(replica_terms[0], 'seq', scatter_dimension=1, tiled=True)]
    all_gather x1 -> x0, blocking collectives: 46.7 us -> none  [local(): lax.all_gather(temporal_kernel, 'seq', axis=1, tiled=True)]
    unnamed x5 -> x0, waiting for transfers between devices: 42.1 us -> none
    all_to_all x4 -> x0, starting transfers between devices: 18.3 us -> none  [the longest x1 5.87 us: local(): lax.all_to_all(out_cotangent, 'seq', split_axis=2, concat_axis=1, tiled=T...]
    all_to_all x4 -> x0, waiting for transfers between devices: 12.9 us -> none  [the longest x1 8.12 us: local(): lax.all_to_all(activated, 'seq', split_axis=2, concat_axis=1, tiled=True)]
  transfers between devices with their start and end apart: 8 -> 0, of which waited for: 5 -> 0; matrix products, arithmetic and copies ran while one was open for 19% -> 0% of each run, Pallas kernels for 0% -> 0%
where the time goes in v1:
time: 125 us
  Pallas kernels  119 us (95%)
  local copies, waits for them, and re-layouts  5.46 us (4%)
    pallas_call x1, Pallas kernels, local(): pl.pallas_call(body, out_shape=(jax.ShapeDtypeStruct(image, BF16), jax.Sh...  119 us
    unnamed x10, local copies, waits for them, and re-layouts  5.46 us

profile of v1, /device:TPU:1, one launch (start us, length us, event | category | flops | bytes accessed | tf_op | source)
XLA Modules:
  0.0 125.3 jit_solution(3099251553787613410)
XLA Ops:
  0.6 119.2 %block.1 = (bf16[16,320,128]{2,1,0:T(8,128)(2,1)}, bf16[16,320,128]{2,1,0:T(8,128)(2,1)}, f32[9,40,320]{2,1,0:T(8,128)}, f32[3,40,320]{2,1,0:T(8,128)}) custom-call(bf16[16,320,128]{2,1,0:T(8,128)(2,1)} %bitcast.4, bf16[9,40,320]{2,1,0:T(8,128)(2,1)} %spatial_ref.1, bf16[3,40,320]{2,1,0:T(8,128)(2,1)} %temporal_ref.1, bf16[16,320,128]{2,1,0:T(8,128)(2,1)} %bitcast.5), custom_call_target="tpu_custom_call" | custom-call | tf_op jit(solution)/shard_map/block/pallas_call | solution.py:573
  119.8 0.0 copy-start
  119.8 2.6 %copy.12 = bf16[1,1,16,320,128]{4,3,2,1,0:T(8,128)(2,1)} copy(bf16[1,1,16,320,128]{4,3,2,1,0:T(8,128)(2,1)} %bitcast.7) | data formatting | bytes 2621440
  122.4 0.0 copy-done
  122.4 0.0 copy-start.1
  122.4 0.0 copy-start.2
  122.4 1.1 copy.13
  123.5 0.3 copy-done.1
  123.8 0.8 copy.14
  124.6 0.0 copy-done.2
  124.6 0.7 copy.15
Async XLA Ops:
  119.8 2.6 %copy-start = (bf16[16,320,128]{2,1,0:T(8,128)(2,1)S(1)}, bf16[16,320,128]{2,1,0:T(8,128)(2,1)}, u32[]{:S(2)}) copy-start(bf16[16,320,128]{2,1,0:T(8,128)(2,1)} %get-tuple-element.9) | copy-start | bytes 3932164
  122.4 1.4 %copy-start.1 = (f32[9,40,320]{2,1,0:T(8,128)S(1)}, f32[9,40,320]{2,1,0:T(8,128)}, u32[]{:S(2)}) copy-start(f32[9,40,320]{2,1,0:T(8,128)} %get-tuple-element.18) | copy-start | bytes 1382404
  122.4 2.2 %copy-start.2 = (f32[3,40,320]{2,1,0:T(8,128)S(1)}, f32[3,40,320]{2,1,0:T(8,128)}, u32[]{:S(2)}) copy-start(f32[3,40,320]{2,1,0:T(8,128)} %get-tuple-element.19) | copy-start | bytes 460804

commit v2 on v1

--- a/solution.py
+++ b/solution.py
@@ -13,6 +13,7 @@
 SHARD = CH // 8
 SLAB = 3 * CH
 WIDE = 1024
+FINAL = ((1, 0), (3, 0), (1, 1), (3, 1), (2, 0), (2, 1), (0, 1))
 BF16, F32 = jnp.bfloat16, jnp.float32
 
 
@@ -52,7 +53,7 @@
     cot_send, cot_recv, act_send, act_recv,
     wx_send, wx_recv, wz_send, wz_recv, wy_send, wy_recv, wc_send, wc_recv,
     gc_send, gc_recv, gy_send, gy_recv, gz_send, gz_recv, gx_send, gx_recv,
-    gh_send, gh_recv, fz_send, fz_recv, fc_send, fc_recv,
+    gh_send, gh_recv, fz_send, fz_recv,
 ):
     s = lax.axis_index("seq")
     d = lax.axis_index("dp")
@@ -76,6 +77,7 @@
     right = {"seq": jnp.minimum(s + 1, 7), "dp": d}
     left = {"seq": jnp.maximum(s - 1, 0), "dp": d}
     has_right, has_left = s < 7, s > 0
+    busy, quiet = jnp.where(ylo == 0, 1, 3), jnp.where(ylo == 0, 3, 1)
     mine = x // 2 == core
 
     load_frames = pltpu.make_async_copy(frames_hbm, frames, load_sem.at[0])
@@ -88,6 +90,9 @@
         for peer in (along_x(offset), along_y(offset), along_z(offset)):
             pl.semaphore_signal(barrier, inc=1, device_id=peer, device_id_type=MESH)
     pl.semaphore_signal(barrier, inc=1, device_id=partner, device_id_type=MESH)
+    for offset in (1, 2, 3):
+        crossed = device(x, y, (z + offset) % 4, 1 - core)
+        pl.semaphore_signal(barrier, inc=1, device_id=crossed, device_id_type=MESH)
 
     @pl.when(s == 3)
     def _():
@@ -105,7 +110,7 @@
         [temporal_ref[k].astype(F32) for k in range(3)], axis=1
     ).astype(BF16)
 
-    pl.semaphore_wait(barrier, jnp.where(jnp.logical_or(s == 3, s == 4), 11, 10))
+    pl.semaphore_wait(barrier, jnp.where(jnp.logical_or(s == 3, s == 4), 14, 13))
 
     def weight_x(offset):
         return remote(
@@ -129,6 +134,29 @@
             target,
         )
 
+    both = pl.ds(2 * core, 2)
+    for offset in (1, 3, 2):
+        @pl.when((x + 4 - offset) % 4 // 2 == core)
+        def _():
+            weight_x(offset).wait_recv()
+
+    def weight_z(offset):
+        chunk = wall.at[z, ylo, both]
+        return remote(chunk, chunk, wz_send.at[offset], wz_recv.at[offset], along_z(offset))
+
+    def weight_y(q, index):
+        chunk = wall.at[q, ylo, both]
+        target = along_y(quiet if index else busy)
+        return remote(chunk, chunk, wy_send.at[index], wy_recv.at[index], target)
+
+    def weight_core(q, index):
+        chunk = wall.at[q, :, both]
+        return remote(chunk, chunk, wc_send.at[index], wc_recv.at[index], partner)
+
+    for offset in (1, 3, 2):
+        weight_z(offset).start()
+    weight_y(z, 0).start()
+
     load_cot.wait()
 
     def send_cot(pair, carry):
@@ -172,33 +200,11 @@
         cot3[2] = jnp.zeros((ROWS, CH, COLS), BF16)
         act3[2] = jnp.zeros((ROWS, CH, COLS), BF16)
 
-    both = pl.ds(2 * core, 2)
-    for offset in (1, 3, 2):
-        @pl.when((x + 4 - offset) % 4 // 2 == core)
-        def _():
-            weight_x(offset).wait_recv()
-
-    def weight_z(offset):
-        chunk = wall.at[z, ylo, both]
-        return remote(chunk, chunk, wz_send.at[offset], wz_recv.at[offset], along_z(offset))
-
-    def weight_y(q, index):
-        chunk = wall.at[q, ylo, both]
-        target = along_y(jnp.where(q < 2, 1, 3))
-        return remote(chunk, chunk, wy_send.at[index], wy_recv.at[index], target)
-
-    def weight_core(q, index):
-        chunk = wall.at[q, :, both]
-        return remote(chunk, chunk, wc_send.at[index], wc_recv.at[index], partner)
-
-    for offset in (1, 3, 2):
-        weight_z(offset).start()
     order = (0, 1, 3, 2)
     for index in order:
-        q = (z + 4 - index) % 4
         if index:
             weight_z(index).wait_recv()
-        weight_y(q, index).start()
+            weight_y((z + 4 - index) % 4, index).start()
     for index in order:
         weight_y((z + 4 - index) % 4, index).wait_recv()
         weight_core((z + 4 - index) % 4, index).start()
@@ -210,13 +216,16 @@
             [wall[q, owner // 4, owner % 4].astype(F32) for owner in range(8)], axis=0
         )
         wl[q] = full.astype(BF16)
-        turned = full.T
+        return carry
+
+    lax.fori_loop(0, 4, place_weights, 0)
+
+    def turn_weights(q, carry):
+        turned = wl[q].astype(F32).T
         wt[q] = jnp.concatenate(
             [turned[CH * a : CH * a + CH] for a in (2, 1, 0)], axis=1
         ).astype(BF16)
         return carry
-
-    lax.fori_loop(0, 4, place_weights, 0)
 
     def slab_pair(ref, pair):
         first = pl.multiple_of(2 * pair * CH, 128)
@@ -255,6 +264,7 @@
         return carry
 
     lax.fori_loop(0, PAIRS, forward, 0)
+    lax.fori_loop(0, 4, turn_weights, 0)
 
     def wait_halo(slots, pair, send, recv):
         @pl.when(has_left)
@@ -340,7 +350,7 @@
         return remote(cs.at[q], cr.at[q], gc_send.at[q], gc_recv.at[q], partner)
 
     def grad_y(q):
-        return remote(ys.at[q], yr.at[q], gy_send.at[q], gy_recv.at[q], along_y(1 if q < 2 else 3))
+        return remote(ys.at[q], yr.at[q], gy_send.at[q], gy_recv.at[q], along_y(quiet))
 
     def grad_z(q):
         offset = (q + 4 - z) % 4
@@ -412,27 +422,19 @@
             hs[...] = total.astype(BF16)
             grad_h.start()
 
-    def final_z(offset):
+    def final_send(offset, cross):
+        target = device(x, y, (z + offset) % 4, core + cross - 2 * core * cross)
         return remote(
-            final.at[z], final.at[z], fz_send.at[offset], fz_recv.at[offset], along_z(offset)
+            final.at[z], final.at[z], fz_send.at[offset, cross], fz_recv.at[offset], target
         )
 
     def h_to_final():
         @pl.when(mine)
         def _():
             grad_h.wait_recv()
-            final[z] = hs[...].astype(F32) + hr[...].astype(F32)
-            for offset in (1, 3, 2):
-                final_z(offset).start()
-
-    final_core = remote(final, final, fc_send.at[0], fc_recv.at[0], partner)
-
-    def final_to_core():
-        @pl.when(mine)
-        def _():
-            for offset in (1, 3, 2):
-                final_z(offset).wait_recv()
-            final_core.start()
+            final[z] = (hs[...].astype(F32) + hr[...].astype(F32)).astype(BF16)
+            for offset, cross in FINAL:
+                final_send(offset, cross).start()
 
     start_core(3)
     spatial_part(0)
@@ -493,24 +495,23 @@
         def _():
             h_to_final()
 
-        @pl.when(pair == 6)
-        def _():
-            final_to_core()
-
         return carry
 
     lax.fori_loop(0, PAIRS, temporal, 0)
+
+    for offset in (1, 3, 2):
+        final_send(offset, 0).wait_recv()
 
     @pl.when(jnp.logical_not(mine))
     def _():
-        final_core.wait_recv()
+        final_send(0, 1).wait_recv()
 
     scale = 1.0 / math.sqrt(16 * 8 * ROWS * COLS)
     for b in range(3):
-        value = final[b] * scale
+        value = final[b].astype(F32) * scale
         for a in range(3):
             sgrad_ref[3 * a + b] = value[:, CH * a : CH * a + CH]
-    value = final[3] * scale
+    value = final[3].astype(F32) * scale
     for slot in range(3):
         tgrad_ref[2 - slot] = jnp.concatenate(
             [
@@ -541,9 +542,9 @@
     def _():
         for offset in (1, 2, 3):
             weight_x(offset).wait_send()
-            final_z(offset).wait_send()
+        for offset, cross in FINAL:
+            final_send(offset, cross).wait_send()
         grad_h.wait_send()
-        final_core.wait_send()
 
     for offset in (1, 2, 3):
         weight_z(offset).wait_send()
@@ -603,7 +604,7 @@
             pltpu.VMEM((4,) + chunk, BF16),
             pltpu.VMEM(chunk, BF16),
             pltpu.VMEM(chunk, BF16),
-            pltpu.VMEM((4,) + chunk, F32),
+            pltpu.VMEM((4,) + chunk, BF16),
             pltpu.VMEM(image, BF16),
             pltpu.VMEM(image, BF16),
             dma((2,)),
@@ -613,7 +614,7 @@
             dma((4,)), dma((4,)), dma((4,)), dma((4,)),
             dma((4,)), dma((4,)), dma((4,)), dma((4,)),
             dma((4,)), dma((4,)), dma((4,)), dma((4,)),
-            dma((1,)), dma((1,)), dma((4,)), dma((4,)), dma((1,)), dma((1,)),
+            dma((1,)), dma((1,)), dma((4, 2)), dma((4,)),
         ],
         compiler_params=pltpu.CompilerParams(
             collective_id=0, has_side_effects=True, vmem_limit_bytes=67043328

time: 125 us -> 114 us (0.912)
  Pallas kernels: 119 us -> 108 us
    pallas_call x1, Pallas kernels: 119 us -> 108 us  [local(): pl.pallas_call(body, out_shape=(jax.ShapeDtypeStruct(image, BF16), jax.Sh...]
where the time goes in v2:
time: 114 us
  Pallas kernels  108 us (95%)
  local copies, waits for them, and re-layouts  5.46 us (5%)
    pallas_call x1, Pallas kernels, local(): pl.pallas_call(body, out_shape=(jax.ShapeDtypeStruct(image, BF16), jax.Sh...  108 us
    unnamed x10, local copies, waits for them, and re-layouts  5.46 us

profile of v2, /device:TPU:1, one launch (start us, length us, event | category | flops | bytes accessed | tf_op | source)
XLA Modules:
  0.0 113.9 jit_solution(3677661758675134431)
XLA Ops:
  0.6 107.8 %block.1 = (bf16[16,320,128]{2,1,0:T(8,128)(2,1)}, bf16[16,320,128]{2,1,0:T(8,128)(2,1)}, f32[9,40,320]{2,1,0:T(8,128)}, f32[3,40,320]{2,1,0:T(8,128)}) custom-call(bf16[16,320,128]{2,1,0:T(8,128)(2,1)} %bitcast.4, bf16[9,40,320]{2,1,0:T(8,128)(2,1)} %spatial_ref.1, bf16[3,40,320]{2,1,0:T(8,128)(2,1)} %temporal_ref.1, bf16[16,320,128]{2,1,0:T(8,128)(2,1)} %bitcast.5), custom_call_target="tpu_custom_call" | custom-call | tf_op jit(solution)/shard_map/block/pallas_call | solution.py:574
  108.4 0.0 copy-start
  108.4 2.6 %copy.12 = bf16[1,1,16,320,128]{4,3,2,1,0:T(8,128)(2,1)} copy(bf16[1,1,16,320,128]{4,3,2,1,0:T(8,128)(2,1)} %bitcast.7) | data formatting | bytes 2621440
  111.0 0.0 copy-done
  111.0 0.0 copy-start.1
  111.0 0.0 copy-start.2
  111.0 1.1 copy.13
  112.0 0.3 copy-done.1
  112.4 0.8 copy.14
  113.2 0.0 copy-done.2
  113.2 0.7 copy.15
Async XLA Ops:
  108.4 2.6 %copy-start = (bf16[16,320,128]{2,1,0:T(8,128)(2,1)S(1)}, bf16[16,320,128]{2,1,0:T(8,128)(2,1)}, u32[]{:S(2)}) copy-start(bf16[16,320,128]{2,1,0:T(8,128)(2,1)} %get-tuple-element.9) | copy-start | bytes 3932164
  111.0 1.4 %copy-start.1 = (f32[9,40,320]{2,1,0:T(8,128)S(1)}, f32[9,40,320]{2,1,0:T(8,128)}, u32[]{:S(2)}) copy-start(f32[9,40,320]{2,1,0:T(8,128)} %get-tuple-element.18) | copy-start | bytes 1382404
  111.0 2.2 %copy-start.2 = (f32[3,40,320]{2,1,0:T(8,128)S(1)}, f32[3,40,320]{2,1,0:T(8,128)}, u32[]{:S(2)}) copy-start(f32[3,40,320]{2,1,0:T(8,128)} %get-tuple-element.19) | copy-start | bytes 460804
